TPU v7x, 32 devices: a whole 2x2x4 slice. The times are simulated.
32 devices in a mesh: groups: 2 (over x), spots: 16 (over z, y, core).
Axes of the slice: x: 2, y: 2, z: 4, core: 2. Of those that a mesh axis runs over, the one named last changes fastest.
Arguments:
- influence: float32 [8, 512, 128, 128], P(None, ('groups', 'spots')), parts along dimension 1, may hold values from 0 to 0.008
- spot_weights: float32 [16384], P(('groups', 'spots')), parts along dimension 0, may hold values from 0.2 to 2
- vox_block: int32 [8, 512], P(None, ('groups', 'spots')), parts along dimension 1, may hold values from 0 to 63, as said below
- spot_block: int32 [8, 512], P(None, ('groups', 'spots')), parts along dimension 1, may hold values from 0 to 3
- labels: int32 [16384], P(('groups', 'spots')), parts along dimension 0, may hold values from 0 to 7
- importance: float32 [16384], P(('groups', 'spots')), parts along dimension 0, may hold values from 1 to 400
- prescription: float32 [16], P('groups'), parts along dimension 0, may hold values from 0.3 to 1.5
Outputs:
- soft_worst: float32 [16384], P(('groups', 'spots')), parts along dimension 0
- gradient: float32 [16384], P(('groups', 'spots')), parts along dimension 0
There are 2 independent parts, one for each index of `groups`. A program takes and returns all parts, laid end to end along the dimension named above; each array names one. Nothing has to cross between parts.
Inputs may be any that keep to these rules, and one draw needn't show every extreme that they name: `vox_block`: device p of the spots axis holds the stored blocks p * 16 to (p + 1) * 16 - 1; the first of them in each scenario names a voxel block of the owner (p + 16 / 2) mod 16, every other one a voxel block of an owner at most 4 indices from p (no block below 0 or past the end).
All inputs are finite; a program needn't handle non-finite values.
Results may differ from a plain program's by a relative error of at most 0.0003.
Values sent between devices are 32-bit elements; how exact they have to be, the bound alone decides.
A program may use at most 64 MiB of HBM per device.

v0:
```python
import jax
import jax.numpy as jnp
from jax import lax
from jax.sharding import PartitionSpec as P


def per_device(influence, spot_weights, vox_block, spot_block, labels, importance, prescription):
    high = lax.Precision.HIGHEST
    scen_count, slot_count, block_rows, block_cols = influence.shape
    num_dev = lax.axis_size("spots")
    spot_rows = spot_weights.shape[0] // block_cols
    vox_rows = labels.shape[0] // block_rows
    local_weights = spot_weights.reshape(spot_rows, block_cols)
    spot_pick = (spot_block[:, :, None] == jnp.arange(spot_rows, dtype=jnp.int32)).astype(
        jnp.float32
    )
    slot_input = jnp.einsum("snb,bk->snk", spot_pick, local_weights, precision=high)
    slot_dose = jnp.einsum("snvk,snk->snv", influence, slot_input, precision=high)
    scen_ids = jnp.broadcast_to(
        jnp.arange(scen_count, dtype=jnp.int32)[:, None], (scen_count, slot_count)
    )
    partial_value = jnp.zeros((vox_rows * num_dev, scen_count, block_rows), jnp.float32)
    partial_value = partial_value.at[vox_block, scen_ids].add(slot_dose)
    dose_field = lax.psum_scatter(partial_value, "spots", scatter_dimension=0, tiled=True)
    label_rows = labels.reshape(vox_rows, block_rows)
    label_hot = (
        label_rows[None, :, :] == jnp.arange(prescription.shape[0], dtype=jnp.int32)[:, None, None]
    ).astype(jnp.float32)
    target = jnp.sum(label_hot * prescription[:, None, None], axis=0)
    imp_rows = importance.reshape(vox_rows, 1, block_rows)
    excess = dose_field - target[:, None, :]
    score = imp_rows * excess * excess
    top_score = jnp.max(score, axis=1, keepdims=True)
    expo_terms = jnp.exp(score - top_score)
    expo_total = jnp.sum(expo_terms, axis=1, keepdims=True)
    soft_worst = (top_score + jnp.log(expo_total)).reshape(vox_rows * block_rows)
    dose_coef = expo_terms / expo_total * 2.0 * imp_rows * excess
    whole_coef = lax.all_gather(dose_coef, "spots", axis=0, tiled=True)
    slot_coef = whole_coef[vox_block, scen_ids]
    slot_grad = jnp.einsum("snvk,snv->snk", influence, slot_coef, precision=high)
    gradient = jnp.einsum("snb,snk->bk", spot_pick, slot_grad, precision=high)
    return (soft_worst, gradient.reshape(spot_rows * block_cols))


def solution(mesh):
    in_specs = (
        P(None, ("groups", "spots"), None, None),
        P(("groups", "spots")),
        P(None, ("groups", "spots")),
        P(None, ("groups", "spots")),
        P(("groups", "spots")),
        P(("groups", "spots")),
        P("groups"),
    )
    out_specs = (P(("groups", "spots")), P(("groups", "spots")))
    return jax.shard_map(
        per_device, mesh=mesh, in_specs=in_specs, out_specs=out_specs, check_vma=False
    )
```

profile of v0, /device:TPU:0, one launch (start us, length us, event | category | flops | bytes accessed | tf_op | source)
XLA Modules:
  0.0 131.3 jit_solution(533600114814965842)
XLA Ops:
  7.2 0.0 copy-start
  7.2 0.0 copy-start.4
  7.2 0.0 copy-start.5
  7.2 0.0 copy-start.2
  7.2 0.0 reduce-scatter.2.cloned.1.call-start
  7.3 0.7 fusion.6
  8.0 0.1 reshape.47
  8.0 0.0 copy-done
  8.0 0.9 fusion
  9.0 0.0 copy-start.3
  9.0 15.4 %fusion.11 = f32[8,16,1,128]{3,2,1,0:T(1,128)S(1)} fusion(f32[8,16,128,1]{2,3,1,0:T(1,128)S(1)} %bitcast.48, f32[8,16,128,128]{3,2,1,0:T(8,128)} %param.7), kind=kOutput, calls=%fused_computation.27 | convolution fusion | flops 25165824 | bytes 8519680 | tf_op jit(solution)/shard_map/snvk,snk->snv/dot_general | solution.py:18
  24.4 6.7 %scatter_fusion = f32[64,8,128]{2,1,0:T(8,128)S(1)} fusion(f32[64,8,128]{2,1,0:T(8,128)S(1)} %broadcast_in_dim.6, s32[128]{0:T(128)S(1)} %reshape.47, f32[128,128]{1,0:T(8,128)S(1)} %bitcast.45), kind=kCustom, calls=%fused_computation.1 | custom fusion | flops 16384 | bytes 197632 | tf_op jit(solution)/shard_map/scatter-add | solution.py:23
  31.1 0.0 copy-start.1
  31.1 0.7 copy-done.1
  31.8 0.0 reduce-scatter.2.cloned.1.call-update
  31.8 0.1 reshape.41
  31.9 0.0 copy-done.4
  31.9 0.0 copy-done.5
  31.9 0.1 select_reduce_fusion
  32.0 0.0 copy-done.2
  32.0 58.4 %reduce-scatter.2.cloned.1.call-done = f32[4,8,128]{2,1,0:T(8,128)} async-done(((f32[64,8,128]{2,1,0:T(8,128)}), f32[4,8,128]{2,1,0:T(8,128)}) %reduce-scatter.2.cloned.1.call-update) | async-done | bytes 16400 | tf_op jit(solution)/shard_map/reduce_scatter | solution.py:24
  90.4 0.7 fusion.2
  91.1 0.7 fusion.1
  91.9 0.6 add_bitcast_fusion
  92.4 0.7 multiply_multiply_fusion.1
  93.2 20.2 %all_gather.3 = f32[64,8,128]{2,1,0:T(8,128)S(1)} all-gather(f32[4,8,128]{2,1,0:T(8,128)S(1)} %multiply_multiply_fusion.1), channel_id=1, replica_groups=mesh['groups'=2,'spots'=16] {'spots'}, dimensions={0}, use_global_device_ids=true | all-gather | bytes 278528 | tf_op jit(solution)/shard_map/all_gather | solution.py:38
  113.3 1.0 gather_fusion
  114.3 9.4 %fusion.12 = f32[8,16,1,128]{3,2,1,0:T(1,128)S(1)} fusion(f32[8,16,128,1]{2,3,1,0:T(1,128)S(1)} %bitcast.46, f32[8,16,128,128]{3,2,1,0:T(8,128)} %param.7), kind=kOutput, calls=%fused_computation.28 | convolution fusion | flops 25165824 | bytes 8519680 | tf_op jit(solution)/shard_map/snvk,snv->snk/dot_general | solution.py:40
  123.7 0.0 copy-done.3
  123.7 0.8 convolution_bitcast_fusion
  (2 shorter events, 0.0 us)
Async XLA Ops:
  7.2 0.9 copy-start
  7.2 24.7 %copy-start.4 = (s32[512]{0:T(512)S(1)}, s32[512]{0:T(512)}, u32[]{:S(2)}) copy-start(s32[512]{0:T(512)} %param.11) | copy-start | bytes 6148
  7.2 24.7 %copy-start.5 = (f32[8]{0:T(128)S(1)}, f32[8]{0:T(128)}, u32[]{:S(2)}) copy-start(f32[8]{0:T(128)} %param.13) | copy-start | bytes 100
  7.2 24.8 %copy-start.2 = (f32[512]{0:T(512)S(1)}, f32[512]{0:T(512)}, u32[]{:S(2)}) copy-start(f32[512]{0:T(512)} %param.12) | copy-start | bytes 6148
  7.2 83.2 %reduce-scatter.2.cloned.1.call-start = ((), (), s32[]{:S(2)}) async-start(), calls=%async_computation.1 | async-start | bytes 278528 | tf_op jit(solution)/shard_map/reduce_scatter | solution.py:24
  9.0 114.7 %copy-start.3 = (s32[8,16]{1,0:T(8,128)S(1)}, s32[8,16]{1,0:T(8,128)}, u32[]{:S(2)}) copy-start(s32[8,16]{1,0:T(8,128)} %param.10) | copy-start | bytes 1540
  31.1 0.7 copy-start.1
Sparse Core Ops, SparseCore 0:
  31.9 58.3 reduce-scatter.1
where the time goes:
time: 132 us; the launch traced here: 131 us
  waiting for transfers between devices  58.4 us (44%)
  matrix products  26.5 us (20%)
  blocking collectives  20.2 us (15%)
  between operations  14.1 us (11%)
  other arithmetic  10.3 us (8%)
  local copies, waits for them, and re-layouts  1.86 us (1%)
    reduce_scatter x1, waiting for transfers between devices, per_device(): lax.psum_scatter(partial_value, 'spots', scatter_dimension=0, tiled=True)  58.4 us
    all_gather x1, blocking collectives, per_device(): whole_coef = lax.all_gather(dose_coef, 'spots', axis=0, tiled=True)  20.2 us
    dot_general x1, matrix products, per_device(): jnp.einsum('snvk,snk->snv', influence, slot_input, precision=high)  15.4 us
    dot_general x1, matrix products, per_device(): jnp.einsum('snvk,snv->snk', influence, slot_coef, precision=high)  9.39 us
    scatter-add x1, other arithmetic, per_device(): partial_value = partial_value.at[vox_block, scen_ids].add(slot_dose)  6.67 us
  transfers between devices with their start and end apart: 1, of which 1 were waited for; matrix products, arithmetic and copies ran while one was open for 0% of the time, Pallas kernels for 0%

commit v1 on v0

v1 whole, which is shorter than its diff:
```python
import functools

import jax
import jax.numpy as jnp
from jax import lax
from jax.experimental import pallas as pl
from jax.experimental.pallas import tpu as pltpu
from jax.sharding import PartitionSpec as P

REACH = 4
NEAR = 2 * REACH + 1
F32 = jnp.float32
BF16 = jnp.bfloat16
MESH = pl.DeviceIdType.MESH


def split(x):
    hi = x.astype(BF16)
    lo = (x - hi.astype(F32)).astype(BF16)
    return hi, lo


def nt_dot(a, b):
    return lax.dot_general(a, b, (((1,), (1,)), ((), ())), preferred_element_type=F32)


def nn_dot(a, b):
    return lax.dot_general(a, b, (((1,), (0,)), ((), ())), preferred_element_type=F32)


def iota(shape, dim):
    return lax.broadcasted_iota(jnp.int32, shape, dim)


def kernel(
    inf_ref, w_ref, vox_ref, spot_ref, lab_ref, imp_ref, presc_ref,
    sw_ref, grad_ref,
    land, ihl, part, recv, coef, cbuf, pick,
    load_sem, send1, recv1, send2, recv2,
):
    scen, slots, rows, cols = land.shape
    vr = lab_ref.shape[0]
    sb = w_ref.shape[0]
    two = 8 // vr
    pairs = scen // two
    dests = NEAR + 1
    qrows = dests * 8
    n = lax.axis_size("spots")
    me = lax.axis_index("spots")
    mirror = lax.rem(me + n // 2, n)

    loads = [
        pltpu.make_async_copy(inf_ref.at[s], land.at[s], load_sem.at[s]) for s in range(scen)
    ]
    for load in loads:
        load.start()

    near = [e for e in range(-REACH, REACH + 1) if e != 0]

    def inside(e):
        return me + e >= 0 if e < 0 else me + e < n

    barrier = pltpu.get_barrier_semaphore()
    for e in near:
        @pl.when(inside(e))
        def _():
            pl.semaphore_signal(barrier, inc=1, device_id={"spots": me + e}, device_id_type=MESH)
    pl.semaphore_signal(barrier, inc=1, device_id={"spots": mirror}, device_id_type=MESH)

    for e in near:
        @pl.when(jnp.logical_not(inside(e)))
        def _():
            recv[e + REACH] = jnp.zeros(recv.shape[1:], F32)
            cbuf[e + REACH] = jnp.zeros(cbuf.shape[1:], F32)

    w_hi, w_lo = split(w_ref[...])
    w_rows = jnp.concatenate([w_hi.astype(F32), w_lo.astype(F32)], axis=0)
    parts = w_rows.shape[0]
    w_two = jnp.concatenate([w_rows, w_rows], axis=1).astype(BF16)

    vox = vox_ref[...]
    slot_id = iota(vox.shape, 1)
    rel = jnp.where(
        slot_id == 0,
        vox - vr * mirror + vr * NEAR,
        vox - vr * me + vr * REACH,
    )
    code = (rel * sb + spot_ref[...]).astype(F32).astype(BF16)
    width = slots * parts
    spread = (iota((slots, width), 1) // parts == iota((slots, width), 0)).astype(F32).astype(BF16)
    spread_t = (iota((width, slots), 0) // parts == iota((width, slots), 1)).astype(F32).astype(BF16)
    key = nn_dot(code, spread).astype(jnp.int32) - iota((scen, width), 1) % sb
    key_t = nt_dot(spread_t, code).astype(jnp.int32) - iota((width, scen), 0) % sb

    far = sb * vr * dests * 2

    def rel_of(q):
        return sb * ((q // 8) * vr + q % vr) + far * ((q % 8) // vr)

    q_id = iota((qrows, two * width), 0)
    row_code = rel_of(q_id)

    for sp in range(pairs):
        outs = []
        for s2 in range(two):
            s = sp * two + s2
            loads[s].wait()
            for b in range(slots):
                hi, lo = split(land[s, b])
                ihl[s, pl.ds(b * rows, rows), pl.ds(0, cols)] = hi
                ihl[s, pl.ds(b * rows, rows), pl.ds(cols, cols)] = lo
                outs.append(nt_dot(w_two, jnp.concatenate([hi, lo], axis=1)))
        dose = jnp.concatenate(outs, axis=0)
        key_row = jnp.concatenate(
            [key[sp * two + s2:sp * two + s2 + 1] + far * s2 for s2 in range(two)], axis=1
        )
        onto = (row_code == key_row).astype(F32).astype(BF16)
        d1 = dose.astype(BF16)
        rest = dose - d1.astype(F32)
        d2, d3 = split(rest)
        total = nn_dot(onto, d1) + (nn_dot(onto, d2) + nn_dot(onto, d3))
        part[:, sp] = total.reshape(dests, 8, rows)

    def copy_of(src, dst, send, rec, e):
        i = REACH + e
        return pltpu.make_async_remote_copy(
            src_ref=src(i), dst_ref=dst.at[REACH - e],
            send_sem=send.at[i], recv_sem=rec.at[REACH - e],
            device_id={"spots": me + e}, device_id_type=MESH,
        )

    def far_copy(src, dst, send, rec):
        return pltpu.make_async_remote_copy(
            src_ref=src(NEAR), dst_ref=dst.at[NEAR],
            send_sem=send.at[NEAR], recv_sem=rec.at[NEAR],
            device_id={"spots": mirror}, device_id_type=MESH,
        )

    def got(dst, send, rec, src, e):
        i = REACH + e
        return pltpu.make_async_remote_copy(
            src_ref=src(i), dst_ref=dst.at[i],
            send_sem=send.at[i], recv_sem=rec.at[i],
            device_id={"spots": me + e}, device_id_type=MESH,
        )

    expected = jnp.int32(1)
    for e in near:
        expected = expected + inside(e).astype(jnp.int32)
    pl.semaphore_wait(barrier, expected)

    order = sorted(near, key=lambda e: -abs(e))

    def exchange(src, dst, send, rec):
        far_copy(src, dst, send, rec).start()
        for e in order:
            @pl.when(inside(e))
            def _():
                copy_of(src, dst, send, rec, e).start()

    def arrive(src, dst, send, rec):
        for e in near:
            @pl.when(inside(e))
            def _():
                got(dst, send, rec, src, e).wait_recv()
        far_copy(src, dst, send, rec).wait_recv()

    def leave(src, dst, send, rec):
        for e in near:
            @pl.when(inside(e))
            def _():
                copy_of(src, dst, send, rec, e).wait_send()
        far_copy(src, dst, send, rec).wait_send()

    from_part = lambda i: part.at[i]
    from_coef = lambda i: coef
    exchange(from_part, recv, send1, recv1)

    lane = iota((width, 2 * 128), 1)
    line = iota((width, 2 * 128), 0)
    q = lane % 128
    lane_code = jnp.where(
        jnp.logical_and(lane // 128 == (line % parts) // sb, q < qrows), rel_of(q), -1000
    )
    for s in range(scen):
        pick[s] = (key_t[:, s:s + 1] + far * (s % two) == lane_code).astype(F32).astype(BF16)
    labels = lab_ref[...]
    target = jnp.zeros(labels.shape, F32)
    for k in range(presc_ref.shape[0]):
        target = jnp.where(labels == k, presc_ref[k], target)
    target = jnp.concatenate([target] * two, axis=0)
    imp = jnp.concatenate([imp_ref[...]] * two, axis=0)

    arrive(from_part, recv, send1, recv1)
    field = part[REACH]
    for i in range(dests):
        if i != REACH:
            field = field + recv[i]
    excess = field - target[None]
    score = imp[None] * excess * excess
    top = jnp.max(score, axis=0)
    top = jnp.maximum(top, pltpu.roll(top, vr, 0))
    expo = jnp.exp(score - top[None])
    whole = jnp.sum(expo, axis=0)
    whole = whole + pltpu.roll(whole, vr, 0)
    coef_now = expo / whole[None] * 2.0 * imp[None] * excess
    coef[...] = coef_now
    exchange(from_coef, cbuf, send2, recv2)
    sw_ref[...] = (top + jnp.log(whole))[:vr]
    cbuf[REACH] = coef_now

    arrive(from_coef, cbuf, send2, recv2)
    acc = jnp.zeros((parts, 2 * cols), F32)
    pad = jnp.zeros((128 - qrows, rows), BF16)
    for sp in range(pairs):
        c_hi, c_lo = split(cbuf[:, sp].reshape(qrows, rows))
        c_two = jnp.concatenate([c_hi, pad, c_lo, pad], axis=0)
        for s2 in range(two):
            s = sp * two + s2
            tiles = nn_dot(pick[s], c_two)
            left = jnp.concatenate(
                [tiles[b * parts:(b + 1) * parts] for b in range(slots)], axis=1
            ).astype(BF16)
            acc = acc + nn_dot(left, ihl[s])
    acc = acc[:, :cols] + acc[:, cols:]
    grad_ref[...] = acc[:sb] + acc[sb:]

    leave(from_part, recv, send1, recv1)
    leave(from_coef, cbuf, send2, recv2)


def per_device(influence, spot_weights, vox_block, spot_block, labels, importance, prescription):
    scen, slots, rows, cols = influence.shape
    sb = spot_weights.shape[0] // cols
    vr = labels.shape[0] // rows
    assert 8 % vr == 0 and 2 * vr == 8 and scen % 2 == 0 and 2 * sb == 8
    slab = (scen * vr // 8, 8, rows)
    dests = NEAR + 1
    vmem = pl.BlockSpec(memory_space=pltpu.VMEM)
    worst, gradient = pl.pallas_call(
        kernel,
        out_shape=(
            jax.ShapeDtypeStruct((vr, rows), F32),
            jax.ShapeDtypeStruct((sb, cols), F32),
        ),
        in_specs=[pl.BlockSpec(memory_space=pl.ANY)] + [vmem] * 5
        + [pl.BlockSpec(memory_space=pltpu.SMEM)],
        out_specs=(vmem, vmem),
        scratch_shapes=[
            pltpu.VMEM((scen, slots, rows, cols), F32),
            pltpu.VMEM((scen, slots * rows, 2 * cols), BF16),
            pltpu.VMEM((dests,) + slab, F32),
            pltpu.VMEM((dests,) + slab, F32),
            pltpu.VMEM(slab, F32),
            pltpu.VMEM((dests,) + slab, F32),
            pltpu.VMEM((scen, slots * 2 * sb, 256), BF16),
            pltpu.SemaphoreType.DMA((scen,)),
            pltpu.SemaphoreType.DMA((dests,)),
            pltpu.SemaphoreType.DMA((dests,)),
            pltpu.SemaphoreType.DMA((dests,)),
            pltpu.SemaphoreType.DMA((dests,)),
        ],
        compiler_params=pltpu.CompilerParams(
            collective_id=0, has_side_effects=True, vmem_limit_bytes=56 * 1024 * 1024
        ),
    )(
        influence, spot_weights.reshape(sb, cols), vox_block, spot_block,
        labels.reshape(vr, rows), importance.reshape(vr, rows), prescription,
    )
    return worst.reshape(vr * rows), gradient.reshape(sb * cols)


def solution(mesh):
    both = P(("groups", "spots"))
    in_specs = (
        P(None, ("groups", "spots"), None, None),
        both,
        P(None, ("groups", "spots")),
        P(None, ("groups", "spots")),
        both,
        both,
        P("groups"),
    )
    return jax.shard_map(
        per_device, mesh=mesh, in_specs=in_specs, out_specs=(both, both), check_vma=False
    )
```

time: 132 us -> 23.5 us (0.18)
  waiting for transfers between devices: 58.4 us -> 0 us
  matrix products: 26.5 us -> 0 us
  blocking collectives: 20.2 us -> 0 us
  Pallas kernels: 0 us -> 20.1 us
  between operations: 14.1 us -> 0.64 us
  other arithmetic: 10.3 us -> 0 us
    reduce_scatter x1 -> x0, waiting for transfers between devices: 58.4 us -> none  [per_device(): lax.psum_scatter(partial_value, 'spots', scatter_dimension=0, tiled=True)]
    dot_general x4 -> x0, matrix products: 26.5 us -> none  [the longest x1 15.4 us: per_device(): jnp.einsum('snvk,snk->snv', influence, slot_input, precision=high)]
    all_gather x1 -> x0, blocking collectives: 20.2 us -> none  [per_device(): whole_coef = lax.all_gather(dose_coef, 'spots', axis=0, tiled=True)]
    pallas_call x0 -> x1, Pallas kernels: none -> 20.1 us  [per_device(): pl.pallas_call(kernel, out_shape=(jax.ShapeDtypeStruct((vr, rows), F32),...]
    scatter-add x1 -> x0, other arithmetic: 6.67 us -> none  [per_device(): partial_value = partial_value.at[vox_block, scen_ids].add(slot_dose)]
    unnamed x12 -> x2, local copies, waits for them, and re-layouts: 0.71 us -> 2.48 us
  transfers between devices with their start and end apart: 1 -> 0, of which waited for: 1 -> 0; matrix products, arithmetic and copies ran while one was open for 0% -> 0% of each run, Pallas kernels for 0% -> 0%
where the time goes in v1:
time: 23.5 us; the launch traced here: 23.2 us
  Pallas kernels  20.1 us (86%)
  local copies, waits for them, and re-layouts  2.48 us (11%)
  between operations  0.64 us (3%)
    pallas_call x1, Pallas kernels, per_device(): pl.pallas_call(kernel, out_shape=(jax.ShapeDtypeStruct((vr, rows), F32),...  20.1 us
    unnamed x2, local copies, waits for them, and re-layouts  2.48 us

profile of v1, /device:TPU:0, one launch (start us, length us, event | category | flops | bytes accessed | tf_op | source)
XLA Modules:
  0.0 23.2 jit_solution(7174483459349744006)
XLA Ops:
  0.6 20.1 %shard_map.86 = (f32[4,128]{1,0:T(4,128)}, f32[4,128]{1,0:T(4,128)}) custom-call(f32[8,16,128,128]{3,2,1,0:T(8,128)} %inf_ref.1, f32[4,128]{1,0:T(4,128)} %bitcast.5, s32[8,16]{1,0:T(8,128)} %vox_ref.1, s32[8,16]{1,0:T(8,128)} %spot_ref.1, s32[4,128]{1,0:T(4,128)} %bitcast.6, f32[4,128]{1,0:T(4,128)} %bitcast.7, f32[8]{0:T(128)} %presc_ref.1), custom_call_target="tpu_custom_call" | custom-call | tf_op jit(solution)/shard_map/pallas_call | solution.py:240
  20.8 1.2 %copy.11 = f32[512]{0:T(512)} copy(f32[512]{0:T(512)} %bitcast.9) | data formatting | bytes 4096
  22.0 1.2 %copy.12 = f32[512]{0:T(512)} copy(f32[512]{0:T(512)} %bitcast.8) | data formatting | bytes 4096

commit v2 on v1

--- a/solution.py
+++ b/solution.py
@@ -33,8 +33,9 @@
 
 
 def kernel(
-    inf_ref, w_ref, vox_ref, spot_ref, lab_ref, imp_ref, presc_ref,
-    sw_ref, grad_ref,
+    inf_ref, w_in, vox_in, spot_in, lab_in, imp_in, presc_in,
+    out_ref,
+    w_ref, vox_ref, spot_ref, lab_ref, imp_ref, presc_ref, small_sem,
     land, ihl, part, recv, coef, cbuf, pick,
     load_sem, send1, recv1, send2, recv2,
 ):
@@ -52,7 +53,14 @@
     loads = [
         pltpu.make_async_copy(inf_ref.at[s], land.at[s], load_sem.at[s]) for s in range(scen)
     ]
-    for load in loads:
+    small = [
+        pltpu.make_async_copy(src, dst, small_sem.at[i])
+        for i, (src, dst) in enumerate((
+            (w_in, w_ref), (vox_in, vox_ref), (spot_in, spot_ref),
+            (lab_in, lab_ref), (imp_in, imp_ref), (presc_in, presc_ref),
+        ))
+    ]
+    for load in small[:3] + loads + small[3:]:
         load.start()
 
     near = [e for e in range(-REACH, REACH + 1) if e != 0]
@@ -72,6 +80,9 @@
         def _():
             recv[e + REACH] = jnp.zeros(recv.shape[1:], F32)
             cbuf[e + REACH] = jnp.zeros(cbuf.shape[1:], F32)
+
+    for load in small[:3]:
+        load.wait()
 
     w_hi, w_lo = split(w_ref[...])
     w_rows = jnp.concatenate([w_hi.astype(F32), w_lo.astype(F32)], axis=0)
@@ -109,7 +120,8 @@
                 hi, lo = split(land[s, b])
                 ihl[s, pl.ds(b * rows, rows), pl.ds(0, cols)] = hi
                 ihl[s, pl.ds(b * rows, rows), pl.ds(cols, cols)] = lo
-                outs.append(nt_dot(w_two, jnp.concatenate([hi, lo], axis=1)))
+            for b in range(slots):
+                outs.append(nt_dot(w_two, ihl[s, pl.ds(b * rows, rows)]))
         dose = jnp.concatenate(outs, axis=0)
         key_row = jnp.concatenate(
             [key[sp * two + s2:sp * two + s2 + 1] + far * s2 for s2 in range(two)], axis=1
@@ -184,6 +196,8 @@
     )
     for s in range(scen):
         pick[s] = (key_t[:, s:s + 1] + far * (s % two) == lane_code).astype(F32).astype(BF16)
+    for load in small[3:]:
+        load.wait()
     labels = lab_ref[...]
     target = jnp.zeros(labels.shape, F32)
     for k in range(presc_ref.shape[0]):
@@ -206,11 +220,11 @@
     coef_now = expo / whole[None] * 2.0 * imp[None] * excess
     coef[...] = coef_now
     exchange(from_coef, cbuf, send2, recv2)
-    sw_ref[...] = (top + jnp.log(whole))[:vr]
+    out_ref[pl.ds(0, vr)] = (top + jnp.log(whole))[:vr]
     cbuf[REACH] = coef_now
 
     arrive(from_coef, cbuf, send2, recv2)
-    acc = jnp.zeros((parts, 2 * cols), F32)
+    sums = []
     pad = jnp.zeros((128 - qrows, rows), BF16)
     for sp in range(pairs):
         c_hi, c_lo = split(cbuf[:, sp].reshape(qrows, rows))
@@ -221,9 +235,12 @@
             left = jnp.concatenate(
                 [tiles[b * parts:(b + 1) * parts] for b in range(slots)], axis=1
             ).astype(BF16)
-            acc = acc + nn_dot(left, ihl[s])
+            sums.append(nn_dot(left, ihl[s]))
+    while len(sums) > 1:
+        sums = [sums[i] + sums[i + 1] for i in range(0, len(sums), 2)]
+    acc = sums[0]
     acc = acc[:, :cols] + acc[:, cols:]
-    grad_ref[...] = acc[:sb] + acc[sb:]
+    out_ref[pl.ds(vr, sb)] = acc[:sb] + acc[sb:]
 
     leave(from_part, recv, send1, recv1)
     leave(from_coef, cbuf, send2, recv2)
@@ -237,16 +254,19 @@
     slab = (scen * vr // 8, 8, rows)
     dests = NEAR + 1
     vmem = pl.BlockSpec(memory_space=pltpu.VMEM)
-    worst, gradient = pl.pallas_call(
+    both = pl.pallas_call(
         kernel,
-        out_shape=(
-            jax.ShapeDtypeStruct((vr, rows), F32),
-            jax.ShapeDtypeStruct((sb, cols), F32),
-        ),
-        in_specs=[pl.BlockSpec(memory_space=pl.ANY)] + [vmem] * 5
-        + [pl.BlockSpec(memory_space=pltpu.SMEM)],
-        out_specs=(vmem, vmem),
+        out_shape=jax.ShapeDtypeStruct((vr + sb, rows), F32),
+        in_specs=[pl.BlockSpec(memory_space=pl.ANY)] * 7,
+        out_specs=vmem,
         scratch_shapes=[
+            pltpu.VMEM((sb, cols), F32),
+            pltpu.VMEM(vox_block.shape, jnp.int32),
+            pltpu.VMEM(spot_block.shape, jnp.int32),
+            pltpu.VMEM((vr, rows), jnp.int32),
+            pltpu.VMEM((vr, rows), F32),
+            pltpu.SMEM(prescription.shape, F32),
+            pltpu.SemaphoreType.DMA((6,)),
             pltpu.VMEM((scen, slots, rows, cols), F32),
             pltpu.VMEM((scen, slots * rows, 2 * cols), BF16),
             pltpu.VMEM((dests,) + slab, F32),
@@ -267,7 +287,7 @@
         influence, spot_weights.reshape(sb, cols), vox_block, spot_block,
         labels.reshape(vr, rows), importance.reshape(vr, rows), prescription,
     )
-    return worst.reshape(vr * rows), gradient.reshape(sb * cols)
+    return both[:vr].reshape(vr * rows), both[vr:].reshape(sb * cols)
 
 
 def solution(mesh):

time: 23.5 us -> 22.5 us (0.957)
  local copies, waits for them, and re-layouts: 2.48 us -> 1.33 us
    unnamed x2 -> x0, local copies, waits for them, and re-layouts: 2.48 us -> none
    reshape x0 -> x1, local copies, waits for them, and re-layouts: none -> 1.33 us  [per_device(): return (both[:vr].reshape(vr * rows), both[vr:].reshape(sb * cols))]
where the time goes in v2:
time: 22.5 us; the launch traced here: 22.3 us
  Pallas kernels  20.3 us (90%)
  local copies, waits for them, and re-layouts  1.33 us (6%)
  between operations  0.64 us (3%)
    pallas_call x1, Pallas kernels, per_device(): pl.pallas_call(kernel, out_shape=jax.ShapeDtypeStruct((vr + sb, rows), F3...  20.3 us
    reshape x1, local copies, waits for them, and re-layouts, per_device(): return (both[:vr].reshape(vr * rows), both[vr:].reshape(sb * cols))  1.33 us

profile of v2, /device:TPU:0, one launch (start us, length us, event | category | flops | bytes accessed | tf_op | source)
XLA Modules:
  0.0 22.3 jit_solution(6177319116471936095)
XLA Ops:
  0.6 20.3 %shard_map.86 = f32[8,128]{1,0:T(8,128)} custom-call(f32[8,16,128,128]{3,2,1,0:T(8,128)} %inf_ref.1, f32[4,128]{1,0:T(4,128)} %bitcast.7, s32[8,16]{1,0:T(8,128)} %vox_in.1, s32[8,16]{1,0:T(8,128)} %spot_in.1, s32[4,128]{1,0:T(4,128)} %bitcast.8, f32[4,128]{1,0:T(4,128)} %bitcast.9, f32[8]{0:T(128)} %presc_in.1), custom_call_target="tpu_custom_call" | custom-call | tf_op jit(solution)/shard_map/pallas_call | solution.py:257
  21.0 1.3 %slice_bitcast_fusion = (f32[512]{0:T(512)}, f32[512]{0:T(512)}) fusion(f32[8,128]{1,0:T(8,128)} %shard_map.86), kind=kLoop, calls=%fused_computation | loop fusion | bytes 8192 | tf_op jit(solution)/shard_map/reshape | solution.py:290

commit v3 on v2

--- a/solution.py
+++ b/solution.py
@@ -224,21 +224,20 @@
     cbuf[REACH] = coef_now
 
     arrive(from_coef, cbuf, send2, recv2)
-    sums = []
-    pad = jnp.zeros((128 - qrows, rows), BF16)
-    for sp in range(pairs):
+    def back(sp, acc):
         c_hi, c_lo = split(cbuf[:, sp].reshape(qrows, rows))
         c_two = jnp.concatenate([c_hi, pad, c_lo, pad], axis=0)
+        sums = []
         for s2 in range(two):
-            s = sp * two + s2
-            tiles = nn_dot(pick[s], c_two)
+            tiles = nn_dot(pick[sp * two + s2], c_two)
             left = jnp.concatenate(
                 [tiles[b * parts:(b + 1) * parts] for b in range(slots)], axis=1
             ).astype(BF16)
-            sums.append(nn_dot(left, ihl[s]))
-    while len(sums) > 1:
-        sums = [sums[i] + sums[i + 1] for i in range(0, len(sums), 2)]
-    acc = sums[0]
+            sums.append(nn_dot(left, ihl[sp * two + s2]))
+        return acc + (sums[0] + sums[1])
+
+    pad = jnp.zeros((128 - qrows, rows), BF16)
+    acc = lax.fori_loop(0, pairs, back, jnp.zeros((parts, 2 * cols), F32))
     acc = acc[:, :cols] + acc[:, cols:]
     out_ref[pl.ds(vr, sb)] = acc[:sb] + acc[sb:]
 

time: 22.5 us -> 21.3 us (0.947)
  Pallas kernels: 20.3 us -> 19.1 us
    pallas_call x1, Pallas kernels: 20.3 us -> 19.1 us  [per_device(): pl.pallas_call(kernel, out_shape=jax.ShapeDtypeStruct((vr + sb, rows), F3...]
where the time goes in v3:
time: 21.3 us; the launch traced here: 21.1 us
  Pallas kernels  19.1 us (90%)
  local copies, waits for them, and re-layouts  1.33 us (6%)
  between operations  0.64 us (3%)
    pallas_call x1, Pallas kernels, per_device(): pl.pallas_call(kernel, out_shape=jax.ShapeDtypeStruct((vr + sb, rows), F3...  19.1 us
    reshape x1, local copies, waits for them, and re-layouts, per_device(): return (both[:vr].reshape(vr * rows), both[vr:].reshape(sb * cols))  1.33 us

profile of v3, /device:TPU:0, one launch (start us, length us, event | category | flops | bytes accessed | tf_op | source)
XLA Modules:
  0.0 21.1 jit_solution(16029432879378134436)
XLA Ops:
  0.6 19.1 %shard_map.86 = f32[8,128]{1,0:T(8,128)} custom-call(f32[8,16,128,128]{3,2,1,0:T(8,128)} %inf_ref.1, f32[4,128]{1,0:T(4,128)} %bitcast.7, s32[8,16]{1,0:T(8,128)} %vox_in.1, s32[8,16]{1,0:T(8,128)} %spot_in.1, s32[4,128]{1,0:T(4,128)} %bitcast.8, f32[4,128]{1,0:T(4,128)} %bitcast.9, f32[8]{0:T(128)} %presc_in.1), custom_call_target="tpu_custom_call" | custom-call | tf_op jit(solution)/shard_map/pallas_call | solution.py:256
  19.8 1.3 %slice_bitcast_fusion = (f32[512]{0:T(512)}, f32[512]{0:T(512)}) fusion(f32[8,128]{1,0:T(8,128)} %shard_map.86), kind=kLoop, calls=%fused_computation | loop fusion | bytes 8192 | tf_op jit(solution)/shard_map/reshape | solution.py:289
